TPU v7x, 32 devices: a whole 2x2x4 slice. The times are simulated.
32 devices in a mesh: blk: 8 (over y, x, core), lines: 4 (over z).
Axes of the slice: x: 2, y: 2, z: 4, core: 2. Of those that a mesh axis runs over, the one named last changes fastest.
Arguments:
- velocity: float32 [3, 12288, 1024], P(None, 'lines', 'blk'), may hold values from -6 to 6
- metric: float32 [1024], P('blk'), may hold values from 0.5 to 2
Outputs:
- derivs: float32 [3, 12288, 1024], P(None, 'lines', 'blk')
- profile: float32 [1024], P('blk')
All inputs are finite; a program needn't handle non-finite values.
Results may differ from a plain program's by a relative error of at most 0.00007.
Values sent between devices are 32-bit elements; how exact they have to be, the bound alone decides.
No kernel may reach another device: no remote copies, remote signals or barrier semaphores. Data moves between devices by JAX's collectives and lax.ppermute only.
A program may use at most 128 MiB of HBM per device.

v0:
```python
import jax
import jax.numpy as jnp
from jax import lax
from jax.sharding import PartitionSpec as P

ALPHA = 1.0 / 3.0
COEF_A = 7.0 / 9.0
COEF_B = 1.0 / 36.0


def block_inverse(width):
    counter = jnp.arange(width, dtype=jnp.int32) + 1
    product = counter[:, None] * counter[None, :] % (2 * (width + 1))
    angles = jnp.pi / (width + 1.0)
    sines = jnp.sqrt(2.0 / (width + 1.0)) * jnp.sin(angles * product.astype(jnp.float32))
    eigen = 1.0 + 2.0 * ALPHA * jnp.cos(angles * counter.astype(jnp.float32))
    return jnp.dot(sines / eigen[None, :], sines, precision=lax.Precision.HIGHEST)


def solve_rows(source, inverse):
    shape = source.shape
    flat = jnp.dot(source.reshape(-1, shape[-1]), inverse, precision=lax.Precision.HIGHEST)
    return flat.reshape(shape)


def interface(first_own, last_own, last_left, first_right, couple):
    factor = 1.0 / (1.0 - couple * couple)
    last_prev = (last_left - couple * first_own) * factor
    last_here = (last_own - couple * first_right) * factor
    first_next = first_right - couple * last_here
    return (last_prev, first_next)


def correct(partial_value, inverse, last_prev, first_next):
    width = inverse.shape[0]
    return partial_value - ALPHA * (
        last_prev[..., None] * inverse[:, 0] + first_next[..., None] * inverse[:, width - 1]
    )


def local(velocity, metric):
    width = velocity.shape[2]
    inverse = block_inverse(width)
    couple = ALPHA * inverse[0, 0]
    lines_block = lax.all_to_all(velocity, "blk", split_axis=1, concat_axis=2, tiled=True)
    count = lines_block.shape[-1]
    source = COEF_A * (jnp.roll(lines_block, -1, -1) - jnp.roll(lines_block, 1, -1)) + COEF_B * (
        jnp.roll(lines_block, -2, -1) - jnp.roll(lines_block, 2, -1)
    )
    blocks = source.reshape(lines_block.shape[0], lines_block.shape[1], count // width, width)
    partial_value = solve_rows(blocks, inverse)
    first_own = partial_value[..., 0]
    last_own = partial_value[..., width - 1]
    last_prev, first_next = interface(
        first_own, last_own, jnp.roll(last_own, 1, 2), jnp.roll(first_own, -1, 2), couple
    )
    whole = correct(partial_value, inverse, last_prev, first_next).reshape(lines_block.shape)
    solved = lax.all_to_all(whole, "blk", split_axis=2, concat_axis=1, tiled=True)
    derivs = solved * metric
    squares = jnp.sum(derivs * derivs, axis=(0, 1))
    total = lax.psum(squares, "lines")
    profile = total / (velocity.shape[1] * lax.axis_size("lines"))
    return (derivs, profile)


def solution(mesh):
    in_specs = (P(None, "lines", "blk"), P("blk"))
    out_specs = (P(None, "lines", "blk"), P("blk"))
    return jax.shard_map(local, mesh=mesh, in_specs=in_specs, out_specs=out_specs, check_vma=False)
```

profile of v0, /device:TPU:0, one launch (start us, length us, event | category | flops | bytes accessed | tf_op | source)
XLA Modules:
  0.0 224.0 jit_solution(313442755634897913)
XLA Ops:
  0.6 8.7 %copy.19 = f32[3,3072,128]{2,0,1:T(4,128)} copy(f32[3,3072,128]{2,1,0:T(8,128)} %param.2) | data formatting | bytes 9437184 | tf_op args[0]
  9.3 5.2 %all-to-all-start = ((f32[3,3072,128]{2,0,1:T(4,128)}), f32[3,3072,128]{2,0,1:T(4,128)}, u32[]{:S(2)}, u32[]{:S(2)}) async-start(f32[3,3072,128]{2,0,1:T(4,128)} %copy.19), calls=%async_computation | async-start | bytes 12582912 | tf_op jit(solution)/shard_map/all_to_all | solution.py:45
  14.6 0.9 fusion.3
  15.4 0.5 slice.91
  17.9 68.4 %all-to-all-done = f32[3,3072,128]{2,0,1:T(4,128)} async-done(((f32[3,3072,128]{2,0,1:T(4,128)}), f32[3,3072,128]{2,0,1:T(4,128)}, u32[]{:S(2)}, u32[]{:S(2)}) %all-to-all-start) | async-done | bytes 4718624 | tf_op jit(solution)/shard_map/all_to_all | solution.py:45
  86.3 5.3 %copy.20 = f32[3,3072,128]{2,1,0:T(8,128)} copy(f32[3,3072,128]{2,0,1:T(4,128)} %all-to-all-done) | data formatting | bytes 9437184 | tf_op jit(solution)/shard_map/all_to_all | solution.py:45
  91.6 6.1 %copy.21 = f32[3,384,8,128]{1,3,2,0:T(8,128)} copy(f32[3,384,8,128]{3,1,2,0:T(8,128)} %bitcast.50) | data formatting | bytes 9437184 | tf_op jit(solution)/shard_map/all_to_all | solution.py:45
  97.7 0.0 copy-start
  97.7 4.5 %fusion.33 = (f32[3,384,1023]{1,2,0:T(8,128)S(1)}, f32[3,384,1023]{1,2,0:T(8,128)S(1)}) fusion(f32[3,384,1024]{1,2,0:T(8,128)} %bitcast.42), kind=kLoop, calls=%fused_computation.53 | loop fusion | bytes 18855936 | tf_op jit(solution)/shard_map/jit(_roll_static)/slice | solution.py:47
  102.2 0.6 copy-done
  102.8 2.8 %fusion.31 = (f32[3,384,1022]{1,2,0:T(8,128)S(1)}, f32[3,384,1022]{1,2,0:T(8,128)}) fusion(f32[3,384,1024]{1,2,0:T(8,128)S(1)} %bitcast.43), kind=kLoop, calls=%fused_computation.51 | loop fusion | bytes 18837504 | tf_op jit(solution)/shard_map/jit(_roll_static)/slice | solution.py:48
  105.6 6.7 %fusion.1 = f32[3,384,1024]{1,2,0:T(8,128)S(1)} fusion(f32[3,384,1]{1,2,0:T(1,128)S(1)} %get-tuple-element.9, f32[3,384,1023]{1,2,0:T(8,128)S(1)} %get-tuple-element.11, f32[3,384,1023]{1,2,0:T(8,128)S(1)} %get-tuple-element.10, f32[3,384,1]{1,2,0:T(1,128)S(1)} %get-tuple-element.8, f32[3,384,2]{1,2,0:T(2,128)S(1)} %get-tuple-element.5, ...), kind=kLoop, calls=%fused_computation.3 | loop fusion | flops 10616832 | bytes 23592960 | tf_op jit(solution)/shard_map/add | solution.py:47
  112.3 4.7 %fusion.10 = f32[3,384,8,128]{1,3,2,0:T(8,128)S(1)} fusion(f32[3,384,8,128]{1,3,2,0:T(8,128)S(1)} %bitcast.48, f32[128,128]{0,1:T(8,128)S(1)} %fusion.3), kind=kOutput, calls=%fused_computation.15 | convolution fusion | flops 1811939328 | bytes 9502720 | tf_op jit(solution)/shard_map/dot_general | solution.py:22
  117.1 0.1 fusion.29
  117.3 1.0 multiply_subtract_fusion
  118.3 3.2 %copy.26 = f32[3,384,1024]{1,0,2:T(4,128)S(1)} copy(f32[3,384,1024]{1,2,0:T(8,128)S(1)} %bitcast.49) | data formatting | bytes 9437184 | tf_op jit(solution)/shard_map/reshape | solution.py:57
  121.5 74.9 %all_to_all.36 = f32[3,384,1024]{1,0,2:T(4,128)} all-to-all(f32[3,384,1024]{1,0,2:T(4,128)S(1)} %copy.26), channel_id=1, replica_groups=mesh['blk'=8,'lines'=4] {'blk'}, dimensions={2} | all-to-all | bytes 9437184 | tf_op jit(solution)/shard_map/all_to_all | solution.py:58
  196.4 0.0 copy-start.2
  196.4 6.9 %copy.27 = f32[3,8,384,128]{3,2,1,0:T(8,128)} copy(f32[3,8,384,128]{2,0,3,1:T(4,128)} %bitcast.46) | data formatting | bytes 9437184 | tf_op jit(solution)/shard_map/all_to_all | solution.py:58
  203.3 0.0 copy-done.2
  203.3 0.0 copy-start.1
  203.3 4.9 %multiply_reduce_fusion = f32[128]{0:T(128)S(1)} fusion(f32[3,8,384,128]{2,0,3,1:T(4,128)} %bitcast.47, f32[128]{0:T(128)S(1)} %copy-done.2), kind=kLoop, calls=%fused_computation | loop fusion | flops 3538816 | bytes 4719616 | tf_op jit(solution)/shard_map/reduce_sum | solution.py:60
  208.3 0.0 copy-done.1
  208.3 2.5 %bitcast_multiply_fusion = f32[3,3072,128]{2,1,0:T(8,128)} fusion(f32[3,8,384,128]{3,2,1,0:T(8,128)S(1)} %copy-done.1, f32[128]{0:T(128)S(1)} %copy-done.2), kind=kLoop, calls=%fused_computation.6 | loop fusion | flops 1179648 | bytes 9437696 | tf_op jit(solution)/shard_map/mul | solution.py:59
  210.8 12.7 %psum.7 = f32[128]{0:T(128)S(1)} all-reduce(f32[128]{0:T(128)S(1)} %multiply_reduce_fusion), channel_id=1, replica_groups=mesh['blk'=8,'lines'=4] {'lines'}, use_global_device_ids=true, to_apply=%region_1.2 | all-reduce | flops 128 | bytes 1024 | tf_op jit(solution)/shard_map/psum | solution.py:61
  223.5 0.5 broadcast_multiply_fusion
  (12 shorter events, 0.1 us)
Async XLA Ops:
  9.3 77.0 %all-to-all-start = ((f32[3,3072,128]{2,0,1:T(4,128)}), f32[3,3072,128]{2,0,1:T(4,128)}, u32[]{:S(2)}, u32[]{:S(2)}) async-start(f32[3,3072,128]{2,0,1:T(4,128)} %copy.19), calls=%async_computation | async-start | bytes 12582912 | tf_op jit(solution)/shard_map/all_to_all | solution.py:45
  97.7 5.1 %copy-start = (f32[3,384,8,128]{1,3,2,0:T(8,128)S(1)}, f32[3,384,8,128]{1,3,2,0:T(8,128)}, u32[]{:S(2)}) copy-start(f32[3,384,8,128]{1,3,2,0:T(8,128)} %copy.21) | copy-start | bytes 14155780
  196.4 6.9 %copy-start.2 = (f32[128]{0:T(128)S(1)}, f32[128]{0:T(128)}, u32[]{:S(2)}) copy-start(f32[128]{0:T(128)} %param.3) | copy-start | bytes 1540
  203.3 5.0 %copy-start.1 = (f32[3,8,384,128]{3,2,1,0:T(8,128)S(1)}, f32[3,8,384,128]{3,2,1,0:T(8,128)}, u32[]{:S(2)}) copy-start(f32[3,8,384,128]{3,2,1,0:T(8,128)} %copy.27) | copy-start | bytes 14155780
where the time goes:
time: 225 us; the launch traced here: 224 us
  blocking collectives  87.6 us (39%)
  waiting for transfers between devices  68.4 us (30%)
  local copies, waits for them, and re-layouts  38.7 us (17%)
  other arithmetic  15.8 us (7%)
  matrix products  5.58 us (2%)
  starting transfers between devices  5.17 us (2%)
  between operations  2.74 us (1%)
    all_to_all x1, blocking collectives, local(): lax.all_to_all(whole, 'blk', split_axis=2, concat_axis=1, tiled=True)  74.9 us
    all_to_all x1, waiting for transfers between devices, local(): lax.all_to_all(velocity, 'blk', split_axis=1, concat_axis=2, tiled=True)  68.4 us
    psum x1, blocking collectives, local(): total = lax.psum(squares, 'lines')  12.7 us
    all_to_all x2, local copies, waits for them, and re-layouts, local(): lax.all_to_all(velocity, 'blk', split_axis=1, concat_axis=2, tiled=True)  11.3 us
    unnamed x8, local copies, waits for them, and re-layouts  9.3 us
    all_to_all x1, local copies, waits for them, and re-layouts, local(): lax.all_to_all(whole, 'blk', split_axis=2, concat_axis=1, tiled=True)  6.91 us
    add x1, other arithmetic, local(): COEF_A * (jnp.roll(lines_block, -1, -1) - jnp.roll(lines_block, 1, -1))  6.72 us
    all_to_all x1, starting transfers between devices, local(): lax.all_to_all(velocity, 'blk', split_axis=1, concat_axis=2, tiled=True)  5.17 us
  transfers between devices with their start and end apart: 1, of which 1 were waited for; matrix products, arithmetic and copies ran while one was open for 1% of the time, Pallas kernels for 0%

commit v1 on v0

--- a/solution.py
+++ b/solution.py
@@ -42,7 +42,19 @@
     width = velocity.shape[2]
     inverse = block_inverse(width)
     couple = ALPHA * inverse[0, 0]
-    lines_block = lax.all_to_all(velocity, "blk", split_axis=1, concat_axis=2, tiled=True)
+    ways, here = (lax.axis_size("blk"), lax.axis_index("blk"))
+    width_2 = velocity.shape[1] // ways
+    shape_2 = list(velocity.shape)
+    shape_2[1] = width_2
+    height = shape_2[2]
+    shape_2[2] = height * ways
+    full = jnp.zeros(shape_2, velocity.dtype)
+    for mask in range(ways):
+        part = lax.dynamic_slice_in_dim(velocity, (here ^ mask) * width_2, width_2, axis=1)
+        if mask:
+            part = lax.ppermute(part, "blk", [(d, d ^ mask) for d in range(ways)])
+        full = lax.dynamic_update_slice_in_dim(full, part, (here ^ mask) * height, axis=2)
+    lines_block = full
     count = lines_block.shape[-1]
     source = COEF_A * (jnp.roll(lines_block, -1, -1) - jnp.roll(lines_block, 1, -1)) + COEF_B * (
         jnp.roll(lines_block, -2, -1) - jnp.roll(lines_block, 2, -1)

time: 225 us -> 189 us (0.84)
  waiting for transfers between devices: 68.4 us -> 37.4 us
  local copies, waits for them, and re-layouts: 38.7 us -> 30.1 us
  starting transfers between devices: 5.17 us -> 9.35 us
    all_to_all x1 -> x0, waiting for transfers between devices: 68.4 us -> none  [local(): lax.all_to_all(velocity, 'blk', split_axis=1, concat_axis=2, tiled=True)]
    ppermute x0 -> x7, waiting for transfers between devices: none -> 37.4 us  [local(): part = lax.ppermute(part, 'blk', [(d, d ^ mask) for d in range(ways)])]
    all_to_all x2 -> x0, local copies, waits for them, and re-layouts: 11.3 us -> none  [local(): lax.all_to_all(velocity, 'blk', split_axis=1, concat_axis=2, tiled=True)]
    ppermute x0 -> x7, starting transfers between devices: none -> 9.35 us  [local(): part = lax.ppermute(part, 'blk', [(d, d ^ mask) for d in range(ways)])]
    all_to_all x1 -> x0, starting transfers between devices: 5.17 us -> none  [local(): lax.all_to_all(velocity, 'blk', split_axis=1, concat_axis=2, tiled=True)]
    dynamic_update_slice x0 -> x8, local copies, waits for them, and re-layouts: none -> 4.6 us  [local(): lax.dynamic_update_slice_in_dim(full, part, (here ^ mask) * height, axis=2)]
    slice x2, local copies, waits for them, and re-layouts: 4.52 us -> 0.63 us  [local(): jnp.roll(lines_block, 1, -1)]
    dynamic_slice x0 -> x1, local copies, waits for them, and re-layouts: none -> 3.67 us  [local(): lax.dynamic_slice_in_dim(velocity, (here ^ mask) * width_2, width_2, axis=1)]
  transfers between devices with their start and end apart: 1 -> 7, of which waited for: 1 -> 3; matrix products, arithmetic and copies ran while one was open for 1% -> 6% of each run, Pallas kernels for 0% -> 0%
where the time goes in v1:
time: 189 us
  blocking collectives  87.4 us (46%)
  waiting for transfers between devices  37.4 us (20%)
  local copies, waits for them, and re-layouts  30.1 us (16%)
  other arithmetic  15.8 us (8%)
  starting transfers between devices  9.35 us (5%)
  matrix products  5.58 us (3%)
  between operations  3 us (2%)
    all_to_all x1, blocking collectives, local(): lax.all_to_all(whole, 'blk', split_axis=2, concat_axis=1, tiled=True)  75.4 us
    ppermute x7, waiting for transfers between devices, local(): part = lax.ppermute(part, 'blk', [(d, d ^ mask) for d in range(ways)])  37.4 us
    psum x1, blocking collectives, local(): total = lax.psum(squares, 'lines')  11.9 us
    ppermute x7, starting transfers between devices, local(): part = lax.ppermute(part, 'blk', [(d, d ^ mask) for d in range(ways)])  9.35 us
    unnamed x17, local copies, waits for them, and re-layouts  7.34 us
    all_to_all x1, local copies, waits for them, and re-layouts, local(): lax.all_to_all(whole, 'blk', split_axis=2, concat_axis=1, tiled=True)  6.91 us
    add x1, other arithmetic, local(): COEF_A * (jnp.roll(lines_block, -1, -1) - jnp.roll(lines_block, 1, -1))  6.72 us
    reduce_sum x1, other arithmetic, local(): squares = jnp.sum(derivs * derivs, axis=(0, 1))  4.95 us
  transfers between devices with their start and end apart: 7, of which 3 were waited for; matrix products, arithmetic and copies ran while one was open for 6% of the time, Pallas kernels for 0%

profile of v1, /device:TPU:0, one launch (start us, length us, event | category | flops | bytes accessed | tf_op | source)
XLA Modules:
  0.0 188.7 jit_solution(17824313694933770111)
XLA Ops:
  0.7 3.7 %constant_dynamic-slice_fusion = (f32[3,384,128]{2,1,0:T(8,128)S(1)}, f32[3,384,128]{2,1,0:T(8,128)S(1)}, f32[3,384,128]{2,1,0:T(8,128)S(1)}, f32[3,384,128]{2,1...) fusion(f32[3,3072,128]{2,1,0:T(8,128)} %param.2, ...), kind=kLoop, calls=%fused_computation.42 | loop fusion | bytes 9437216 | tf_op jit(solution)/shard_map/dynamic_slice | solution.py:53
  4.4 2.1 %copy.39 = f32[3,384,128]{1,2,0:T(8,128)} copy(f32[3,384,128]{2,1,0:T(8,128)} %get-tuple-element.18) | data formatting | bytes 1179648
  6.5 0.5 collective-permute-start
  6.9 2.1 %copy.40 = f32[3,384,128]{1,2,0:T(8,128)} copy(f32[3,384,128]{2,1,0:T(8,128)} %get-tuple-element.17) | data formatting | bytes 1179648
  9.1 2.5 %collective-permute-start.1 = (f32[3,384,128]{1,2,0:T(8,128)}, f32[3,384,128]{1,2,0:T(8,128)}, u32[]{:S(2)}, u32[]{:S(2)}) collective-permute-start(f32[3,384,128]{1,2,0:T(8,128)} %copy.40), channel_id=1, source_target_pairs={{0,8},{4,12},{8,0},{12,4},{16,24},{20,28},{24,16},{28,20},{1,9},{5... | collective-permute-start | bytes 1769480 | tf_op jit(solution)/shard_map/ppermute | solution.py:55
  11.5 1.0 copy.41
  12.7 1.0 copy.42
  13.8 1.8 collective-permute-start.3
  15.9 0.9 fusion.3
  16.8 0.5 slice.91
  20.1 0.3 broadcast_in_dim.2
  20.5 2.6 %collective-permute-start.5 = (f32[3,384,128]{1,2,0:T(8,128)S(1)}, f32[3,384,128]{1,2,0:T(8,128)S(1)}, u32[]{:S(2)}, u32[]{:S(2)}) collective-permute-start(f32[3,384,128]{1,2,0:T(8,128)S(1)} %copy.44), channel_id=1, source_target_pairs={{0,24},{4,28},{8,16},{12,20},{16,8},{20,12},{24,0},{28,4},{1,25},{... | collective-permute-start | bytes 1769480 | tf_op jit(solution)/shard_map/ppermute | solution.py:55
  23.1 1.1 constant_dynamic-update-slice_fusion.6
  24.2 1.8 collective-permute-done.1
  26.0 1.8 collective-permute-start.6
  27.9 1.1 constant_dynamic-update-slice_fusion.5
  29.0 9.3 %collective-permute-done.2 = f32[3,384,128]{1,2,0:T(8,128)} collective-permute-done((f32[3,384,128]{1,2,0:T(8,128)}, f32[3,384,128]{1,2,0:T(8,128)}, u32[]{:S(2)}, u32[]{:S(2)}) %collective-permute-start.2) | collective-permute-done | bytes 589856 | tf_op jit(solution)/shard_map/ppermute | solution.py:55
  38.3 1.1 constant_dynamic-update-slice_fusion.4
  39.4 1.1 constant_dynamic-update-slice_fusion.3
  40.5 26.3 %collective-permute-done.4 = f32[3,384,128]{1,2,0:T(8,128)S(1)} collective-permute-done((f32[3,384,128]{1,2,0:T(8,128)S(1)}, f32[3,384,128]{1,2,0:T(8,128)S(1)}, u32[]{:S(2)}, u32[]{:S(2)}) %collective-permute-start.4) | collective-permute-done | bytes 589856 | tf_op jit(solution)/shard_map/ppermute | solution.py:55
  67.0 0.6 fusion.33
  67.6 2.8 %fusion.31 = (f32[3,384,1022]{1,2,0:T(8,128)S(1)}, f32[3,384,1022]{1,2,0:T(8,128)}) fusion(f32[3,384,1024]{1,2,0:T(8,128)S(1)} %constant_dynamic-update-slice_fusion), kind=kLoop, calls=%fused_computation.67 | loop fusion | bytes 18837504 | tf_op jit(solution)/shard_map/jit(_roll_static)/slice | solution.py:60
  70.5 6.7 %fusion.1 = f32[3,384,1024]{1,2,0:T(8,128)S(1)} fusion(f32[3,384,1]{1,2,0:T(1,128)S(1)} %get-tuple-element.9, f32[3,384,1023]{1,2,0:T(8,128)S(1)} %get-tuple-element.11, f32[3,384,1023]{1,2,0:T(8,128)S(1)} %get-tuple-element.10, f32[3,384,1]{1,2,0:T(1,128)S(1)} %get-tuple-element.8, f32[3,384,2]{1,2,0:T(2,128)S(1)} %get-tuple-element.5, ...), kind=kLoop, calls=%fused_computation.3 | loop fusion | flops 10616832 | bytes 23592960 | tf_op jit(solution)/shard_map/add | solution.py:59
  77.2 4.7 %fusion.10 = f32[3,384,8,128]{1,3,2,0:T(8,128)S(1)} fusion(f32[3,384,8,128]{1,3,2,0:T(8,128)S(1)} %bitcast.40, f32[128,128]{0,1:T(8,128)S(1)} %copy-done.2), kind=kOutput, calls=%fused_computation.15 | convolution fusion | flops 1811939328 | bytes 9502720 | tf_op jit(solution)/shard_map/dot_general | solution.py:22
  82.1 1.0 multiply_subtract_fusion
  83.2 3.2 %copy.33 = f32[3,384,1024]{1,0,2:T(4,128)S(1)} copy(f32[3,384,1024]{1,2,0:T(8,128)S(1)} %bitcast.41) | data formatting | bytes 9437184 | tf_op jit(solution)/shard_map/reshape | solution.py:69
  86.4 75.4 %all_to_all.18 = f32[3,384,1024]{1,0,2:T(4,128)} all-to-all(f32[3,384,1024]{1,0,2:T(4,128)S(1)} %copy.33), channel_id=1, replica_groups=mesh['blk'=8,'lines'=4] {'blk'}, dimensions={2} | all-to-all | bytes 9437184 | tf_op jit(solution)/shard_map/all_to_all | solution.py:70
  161.8 6.9 %copy.34 = f32[3,8,384,128]{3,2,1,0:T(8,128)} copy(f32[3,8,384,128]{2,0,3,1:T(4,128)} %bitcast.38) | data formatting | bytes 9437184 | tf_op jit(solution)/shard_map/all_to_all | solution.py:70
  168.8 4.9 %multiply_reduce_fusion = f32[128]{0:T(128)S(1)} fusion(f32[3,8,384,128]{2,0,3,1:T(4,128)} %bitcast.39, f32[128]{0:T(128)S(1)} %copy-done.3), kind=kLoop, calls=%fused_computation | loop fusion | flops 3538816 | bytes 4719616 | tf_op jit(solution)/shard_map/reduce_sum | solution.py:72
  173.7 2.5 %bitcast_multiply_fusion = f32[3,3072,128]{2,1,0:T(8,128)} fusion(f32[3,8,384,128]{3,2,1,0:T(8,128)S(1)} %copy-done, f32[128]{0:T(128)S(1)} %copy-done.3), kind=kLoop, calls=%fused_computation.6 | loop fusion | flops 1179648 | bytes 9437696 | tf_op jit(solution)/shard_map/mul | solution.py:71
  176.2 11.9 %psum.7 = f32[128]{0:T(128)S(1)} all-reduce(f32[128]{0:T(128)S(1)} %multiply_reduce_fusion), channel_id=1, replica_groups=mesh['blk'=8,'lines'=4] {'lines'}, use_global_device_ids=true, to_apply=%region_1.2 | all-reduce | flops 128 | bytes 1024 | tf_op jit(solution)/shard_map/psum | solution.py:73
  188.1 0.5 broadcast_multiply_fusion
  (35 shorter events, 1.6 us)
Async XLA Ops:
  6.5 14.0 %collective-permute-start = (f32[3,384,128]{1,2,0:T(8,128)}, f32[3,384,128]{1,2,0:T(8,128)}, u32[]{:S(2)}, u32[]{:S(2)}) collective-permute-start(f32[3,384,128]{1,2,0:T(8,128)} %copy.39), channel_id=1, source_target_pairs={{0,4},{4,0},{8,12},{12,8},{16,20},{20,16},{24,28},{28,24},{1,5},{5... | collective-permute-start | bytes 1769480 | tf_op jit(solution)/shard_map/ppermute | solution.py:55
  9.1 17.0 %collective-permute-start.1 = (f32[3,384,128]{1,2,0:T(8,128)}, f32[3,384,128]{1,2,0:T(8,128)}, u32[]{:S(2)}, u32[]{:S(2)}) collective-permute-start(f32[3,384,128]{1,2,0:T(8,128)} %copy.40), channel_id=1, source_target_pairs={{0,8},{4,12},{8,0},{12,4},{16,24},{20,28},{24,16},{28,20},{1,9},{5... | collective-permute-start | bytes 1769480 | tf_op jit(solution)/shard_map/ppermute | solution.py:55
  12.6 25.7 %collective-permute-start.2 = (f32[3,384,128]{1,2,0:T(8,128)}, f32[3,384,128]{1,2,0:T(8,128)}, u32[]{:S(2)}, u32[]{:S(2)}) collective-permute-start(f32[3,384,128]{1,2,0:T(8,128)} %copy.41), channel_id=1, source_target_pairs={{0,12},{4,8},{8,4},{12,0},{16,28},{20,24},{24,20},{28,16},{1,13},{... | collective-permute-start | bytes 1769480 | tf_op jit(solution)/shard_map/ppermute | solution.py:55
  13.8 25.7 %collective-permute-start.3 = (f32[3,384,128]{1,2,0:T(8,128)}, f32[3,384,128]{1,2,0:T(8,128)}, u32[]{:S(2)}, u32[]{:S(2)}) collective-permute-start(f32[3,384,128]{1,2,0:T(8,128)} %copy.42), channel_id=1, source_target_pairs={{0,16},{4,20},{8,24},{12,28},{16,0},{20,4},{24,8},{28,12},{1,17},{... | collective-permute-start | bytes 1769480 | tf_op jit(solution)/shard_map/ppermute | solution.py:55
  15.8 51.1 %collective-permute-start.4 = (f32[3,384,128]{1,2,0:T(8,128)S(1)}, f32[3,384,128]{1,2,0:T(8,128)S(1)}, u32[]{:S(2)}, u32[]{:S(2)}) collective-permute-start(f32[3,384,128]{1,2,0:T(8,128)S(1)} %copy.43), channel_id=1, source_target_pairs={{0,20},{4,16},{8,28},{12,24},{16,4},{20,0},{24,12},{28,8},{1,21},{... | collective-permute-start | bytes 1769480 | tf_op jit(solution)/shard_map/ppermute | solution.py:55
  16.7 0.6 copy-start.1
  20.5 46.4 %collective-permute-start.5 = (f32[3,384,128]{1,2,0:T(8,128)S(1)}, f32[3,384,128]{1,2,0:T(8,128)S(1)}, u32[]{:S(2)}, u32[]{:S(2)}) collective-permute-start(f32[3,384,128]{1,2,0:T(8,128)S(1)} %copy.44), channel_id=1, source_target_pairs={{0,24},{4,28},{8,16},{12,20},{16,8},{20,12},{24,0},{28,4},{1,25},{... | collective-permute-start | bytes 1769480 | tf_op jit(solution)/shard_map/ppermute | solution.py:55
  26.0 40.9 %collective-permute-start.6 = (f32[3,384,128]{1,2,0:T(8,128)S(1)}, f32[3,384,128]{1,2,0:T(8,128)S(1)}, u32[]{:S(2)}, u32[]{:S(2)}) collective-permute-start(f32[3,384,128]{1,2,0:T(8,128)S(1)} %copy.45), channel_id=1, source_target_pairs={{0,28},{4,24},{8,20},{12,16},{16,12},{20,8},{24,4},{28,0},{1,29},{... | collective-permute-start | bytes 1769480 | tf_op jit(solution)/shard_map/ppermute | solution.py:55
  70.5 6.7 %copy-start.2 = (f32[128,128]{0,1:T(8,128)S(1)}, f32[128,128]{0,1:T(8,128)}, u32[]{:S(2)}) copy-start(f32[128,128]{0,1:T(8,128)} %copy-done.1) | copy-start | bytes 196612
  161.8 6.9 %copy-start.3 = (f32[128]{0:T(128)S(1)}, f32[128]{0:T(128)}, u32[]{:S(2)}) copy-start(f32[128]{0:T(128)} %param.3) | copy-start | bytes 1540
  168.8 5.0 %copy-start = (f32[3,8,384,128]{3,2,1,0:T(8,128)S(1)}, f32[3,8,384,128]{3,2,1,0:T(8,128)}, u32[]{:S(2)}) copy-start(f32[3,8,384,128]{3,2,1,0:T(8,128)} %copy.34) | copy-start | bytes 14155780
